TPU v7x, 256 devices: a whole 4x4x8 slice. The times are simulated.
256 devices in a mesh: pair: 2 (over x_hi), blk: 32 (over x_lo, z, core), rows: 4 (over y).
Axes of the slice: x: 4 (x_hi: 2, x_lo: 2; x = x_hi * 2 + x_lo), y: 4, z: 8, core: 2. Of those that a mesh axis runs over, the one named last changes fastest.
Arguments:
- tiles: float32 [2, 2048, 131072], P('pair', None, ('blk', 'rows')), may hold values from -0.0625 to 0.0625
- trial: float32 [2, 131072, 1024], P('pair', ('blk', 'rows')), may hold values from -6 to 6
Outputs:
- products: float32 [2, 2048, 1024], P('pair', ('blk', 'rows'))
All inputs are finite; a program needn't handle non-finite values.
Results may differ from a plain program's by a relative error of at most 0.000076.
Values sent between devices are 32-bit elements; how exact they have to be, the bound alone decides.
A program may use at most 128 MiB of HBM per device.

v0:
```python
import jax
import jax.numpy as jnp
from jax import lax
from jax.sharding import Mesh
from jax.sharding import PartitionSpec as P

BLK_ROWS = ("blk_0", "blk_1", "blk_2", "rows")


def swapped(value, axis, apart):
    mask = 2**apart
    pairs = [(source, source ^ mask) for source in range(lax.axis_size(axis))]
    return lax.ppermute(value, axis, pairs)


def own_block_2(pieces, axes, turns):
    inside = pieces.shape[1:]
    pieces = pieces.reshape(*(lax.axis_size(a) for a in axes), *inside)
    pieces = jnp.moveaxis(pieces, turns, range(len(axes))).reshape(-1, *inside)
    for k in turns:
        pieces = lax.psum_scatter(pieces, axes[k], scatter_dimension=0, tiled=True)
    return pieces[0]


def in_blocks(array, dim, devices):
    before, after = (array.shape[:dim], array.shape[dim + 1 :])
    return jnp.moveaxis(array.reshape(*before, devices, -1, *after), dim, 0)


def sum_by_axis_2(array, axes, turns, dim):
    devices = lax.axis_size(axes)
    return own_block_2(in_blocks(array, dim, devices), axes, turns)


def shards(tiles, trial):
    own_block = trial[0]
    partner_block = swapped(own_block, "pair", 0)
    parity_sign = 1.0 - 2.0 * lax.axis_index("pair").astype(jnp.float32)
    combined = partner_block + parity_sign * own_block
    matrix = tiles[0]
    local_rows = sum_by_axis_2(
        jnp.dot(
            matrix, combined, precision=lax.Precision.HIGHEST, preferred_element_type=jnp.float32
        ),
        BLK_ROWS,
        (2, 1, 3, 0),
        0,
    )
    partner_rows = swapped(local_rows, "pair", 0)
    result = 0.5 * (partner_rows + parity_sign * local_rows)
    return result[None]


def solution(mesh):
    split = Mesh(
        mesh.devices.reshape(mesh.shape["pair"], 2, 8, 2, mesh.shape["rows"]),
        ("pair", "blk_0", "blk_1", "blk_2", "rows"),
    )
    in_specs = (P("pair", None, BLK_ROWS), P("pair", BLK_ROWS, None))
    out_specs = P("pair", BLK_ROWS, None)
    return jax.shard_map(
        shards, mesh=split, in_specs=in_specs, out_specs=out_specs, check_vma=False
    )
```

profile of v0, /device:TPU:8, one launch (start us, length us, event | category | flops | bytes accessed | tf_op | source)
XLA Modules:
  0.0 317.0 jit_solution(2145282977093574732)
XLA Ops:
  6.5 0.0 reduce-scatter.5.cloned.1.call-start
  6.5 3.0 collective-permute-start
  9.6 91.1 %collective-permute-done = f32[1024,1024]{1,0:T(8,128)} collective-permute-done((f32[1024,1024]{1,0:T(8,128)}, f32[1024,1024]{1,0:T(8,128)}, u32[]{:S(2)}, u32[]{:S(2)}) %collective-permute-start) | collective-permute-done | bytes 4194336 | tf_op jit(solution)/shard_map/ppermute | solution.py:13
  100.7 57.8 %fusion.2 = f32[2048,1024]{0,1:T(8,128)} fusion(f32[1,2048,1024]{2,1,0:T(8,128)} %param.2, f32[1024,1024]{1,0:T(8,128)} %collective-permute-done, f32[]{:T(128)S(6)} %sub.3, f32[1,1024,1024]{2,1,0:T(8,128)} %param.3), kind=kOutput, calls=%fused_computation.2 | convolution fusion | flops 25771900928 | bytes 25165828 | tf_op jit(solution)/shard_map/dot_general | solution.py:42
  158.4 9.3 %copy.5 = f32[2048,1024]{1,0:T(8,128)} copy(f32[2048,1024]{0,1:T(8,128)} %fusion.2) | data formatting | bytes 16777216 | tf_op jit(solution)/shard_map/dot_general | solution.py:42
  167.7 8.3 %copy.6 = f32[2,8,4,2,16,1024]{5,4,3,2,1,0:T(8,128)} copy(f32[2,8,4,2,16,1024]{5,4,2,0,1,3:T(8,128)} %bitcast.21) | data formatting | bytes 16777216 | tf_op jit(solution)/shard_map/transpose | solution.py:19
  176.0 0.0 reduce-scatter.5.cloned.1.call-update
  176.0 0.0 reduce-scatter.7.cloned.1.call-start
  176.0 24.8 %reduce-scatter.5.cloned.1.call-done = f32[64,16,1024]{2,1,0:T(8,128)} async-done(((f32[128,16,1024]{2,1,0:T(8,128)}), f32[64,16,1024]{2,1,0:T(8,128)}) %reduce-scatter.5.cloned.1.call-update) | async-done | bytes 4194320 | tf_op jit(solution)/shard_map/reduce_scatter | solution.py:21
  200.8 0.0 reduce-scatter.7.cloned.1.call-update
  200.9 0.0 reduce-scatter.9.cloned.1.call-start
  200.9 59.1 %reduce-scatter.7.cloned.1.call-done = f32[8,16,1024]{2,1,0:T(8,128)} async-done(((f32[64,16,1024]{2,1,0:T(8,128)}), f32[8,16,1024]{2,1,0:T(8,128)}) %reduce-scatter.7.cloned.1.call-update) | async-done | bytes 524304 | tf_op jit(solution)/shard_map/reduce_scatter | solution.py:21
  260.0 0.0 reduce-scatter.9.cloned.1.call-update
  260.0 0.0 reduce-scatter.11.cloned.1.call-start
  260.1 23.3 %reduce-scatter.9.cloned.1.call-done = f32[2,16,1024]{2,1,0:T(8,128)} async-done(((f32[8,16,1024]{2,1,0:T(8,128)}), f32[2,16,1024]{2,1,0:T(8,128)}) %reduce-scatter.9.cloned.1.call-update) | async-done | bytes 131088 | tf_op jit(solution)/shard_map/reduce_scatter | solution.py:21
  283.4 0.0 reduce-scatter.11.cloned.1.call-update
  283.4 19.6 %reduce-scatter.11.cloned.1.call-done = f32[1,16,1024]{2,1,0:T(8,128)} async-done(((f32[2,16,1024]{2,1,0:T(8,128)}), f32[1,16,1024]{2,1,0:T(8,128)}) %reduce-scatter.11.cloned.1.call-update) | async-done | bytes 65552 | tf_op jit(solution)/shard_map/reduce_scatter | solution.py:21
  303.0 2.7 collective-permute-start.1
  305.7 3.3 %collective-permute-done.1 = f32[16,1024]{1,0:T(8,128)S(1)} collective-permute-done((f32[16,1024]{1,0:T(8,128)}, f32[16,1024]{1,0:T(8,128)S(1)}, u32[]{:S(2)}, u32[]{:S(2)}) %collective-permute-start.1) | collective-permute-done | bytes 65568 | tf_op jit(solution)/shard_map/ppermute | solution.py:13
  309.0 1.5 multiply_bitcast_fusion
Async XLA Ops:
  6.5 194.3 %reduce-scatter.5.cloned.1.call-start = ((), (), s32[]{:S(2)}) async-start(), calls=%async_computation.4 | async-start | bytes 12582912 | tf_op jit(solution)/shard_map/reduce_scatter | solution.py:21
  6.5 94.1 %collective-permute-start = (f32[1024,1024]{1,0:T(8,128)}, f32[1024,1024]{1,0:T(8,128)}, u32[]{:S(2)}, u32[]{:S(2)}) collective-permute-start(f32[1024,1024]{1,0:T(8,128)} %bitcast.23), channel_id=1, source_target_pairs={{0,128},{128,0},{1,129},{129,1},{2,130},{130,2},{3,131},{131,3},{4... | collective-permute-start | bytes 12582920 | tf_op jit(solution)/shard_map/ppermute | solution.py:13
  176.0 84.0 %reduce-scatter.7.cloned.1.call-start = ((), (), s32[]{:S(2)}) async-start(), calls=%async_computation.5 | async-start | bytes 4718592 | tf_op jit(solution)/shard_map/reduce_scatter | solution.py:21
  200.9 82.5 %reduce-scatter.9.cloned.1.call-start = ((), (), s32[]{:S(2)}) async-start(), calls=%async_computation.6 | async-start | bytes 655360 | tf_op jit(solution)/shard_map/reduce_scatter | solution.py:21
  260.0 42.9 %reduce-scatter.11.cloned.1.call-start = ((), (), s32[]{:S(2)}) async-start(), calls=%async_computation.7 | async-start | bytes 196608 | tf_op jit(solution)/shard_map/reduce_scatter | solution.py:21
  303.0 6.0 %collective-permute-start.1 = (f32[16,1024]{1,0:T(8,128)}, f32[16,1024]{1,0:T(8,128)S(1)}, u32[]{:S(2)}, u32[]{:S(2)}) collective-permute-start(f32[16,1024]{1,0:T(8,128)} %bitcast.22), channel_id=1, source_target_pairs={{0,128},{128,0},{1,129},{129,1},{2,130},{130,2},{3,131},{131,3},{4... | collective-permute-start | bytes 196616 | tf_op jit(solution)/shard_map/ppermute | solution.py:13
Sparse Core Ops, SparseCore 0:
  176.1 24.7 reduce-scatter.4
  203.4 56.5 reduce-scatter.6
  262.6 20.7 reduce-scatter.8
  285.7 17.2 reduce-scatter.10
where the time goes:
time: 317 us
  waiting for transfers between devices  221 us (70%)
  matrix products  57.8 us (18%)
  local copies, waits for them, and re-layouts  17.5 us (6%)
  between operations  13.1 us (4%)
  starting transfers between devices  5.83 us (2%)
    reduce_scatter x4, waiting for transfers between devices, own_block_2(): pieces = lax.psum_scatter(pieces, axes[k], scatter_dimension=0, tiled=True)  127 us
    ppermute x2, waiting for transfers between devices, swapped(): return lax.ppermute(value, axis, pairs)  94.4 us
    dot_general x1, matrix products, shards(): jnp.dot(matrix, combined, precision=lax.Precision.HIGHEST, preferred_elem...  57.8 us
    dot_general x1, local copies, waits for them, and re-layouts, shards(): jnp.dot(matrix, combined, precision=lax.Precision.HIGHEST, preferred_elem...  9.25 us
    transpose x1, local copies, waits for them, and re-layouts, own_block_2(): pieces = jnp.moveaxis(pieces, turns, range(len(axes))).reshape(-1, *inside)  8.27 us
  transfers between devices with their start and end apart: 6, of which 6 were waited for; matrix products, arithmetic and copies ran while one was open for 0% of the time, Pallas kernels for 0%

commit v1 on v0

v1 whole, which is shorter than its diff:
```python
import functools

import jax
import jax.numpy as jnp
from jax import lax
from jax.experimental import pallas as pl
from jax.experimental.pallas import tpu as pltpu
from jax.sharding import Mesh
from jax.sharding import PartitionSpec as P

MESH = pl.DeviceIdType.MESH
AXES = ("pair", "xlo", "z", "core", "y")
OWNERS = ("xlo", "z", "core", "y")
LANES = 128
ROWS_AT_ONCE = 512
STAGED = 256


def kernel(
    n_z, n_y, rows, relay,
    a_hbm, x_hbm, out_ref,
    xv, yv, passing, a_hi, a_lo, staged, b_parts,
    prod, core_in, y_in, s2, z_in, s3, far_in,
    x_sem, a_sem, own_send, pass_recv, fwd_send, fwd_recv,
    core_send, core_recv, y_send, y_recv, z_send, z_recv, far_send, far_recv,
):
    p, xlo, z, core, y = (lax.axis_index(a) for a in AXES)
    chunks = xv.shape[0]
    depth, width = a_hbm.shape[1], a_hbm.shape[0]
    half = depth // 2
    x_at = 2 * p + xlo
    sign = 1.0 - 2.0 * p.astype(jnp.float32)

    def along_x(step):
        there = lax.rem(x_at + step + 4, 4)
        return {"pair": there // 2, "xlo": lax.rem(there, 2)}

    right, left = along_x(1), along_x(-1)
    partner = {"pair": 1 - p}
    sibling = {"core": 1 - core}
    y_peers = [{"y": lax.rem(y + d, n_y)} for d in range(1, n_y)]
    z_peers = [{"z": lax.rem(z + d, n_z)} for d in range(1, n_z)]
    far_peers = [
        {"xlo": 1 - xlo},
        {"pair": 1 - p},
        {"pair": 1 - p, "xlo": 1 - xlo},
    ]
    peers = [sibling, *y_peers, *z_peers, *far_peers]

    barrier = pltpu.get_barrier_semaphore()
    for peer in peers:
        pl.semaphore_signal(barrier, inc=1, device_id=peer, device_id_type=MESH)

    def columns(j):
        return pl.ds(pl.multiple_of(j * LANES, LANES), LANES)

    def x_load(j):
        return pltpu.make_async_copy(x_hbm.at[:, columns(j)], xv.at[j], x_sem.at[j])

    def a_load(i):
        slot = lax.rem(i, 2)
        return pltpu.make_async_copy(
            a_hbm.at[pl.ds(pl.multiple_of(i * STAGED, STAGED), STAGED)], staged.at[slot], a_sem.at[slot]
        )

    def remote(src, dst, send, recv, peer):
        return pltpu.make_async_remote_copy(
            src_ref=src, dst_ref=dst, send_sem=send, recv_sem=recv, device_id=peer, device_id_type=MESH
        )

    ways = ((0, right), (1, left))

    def own(j, way, peer):
        return remote(
            x_hbm.at[pl.ds(way * half, half), columns(j)],
            passing.at[j, way],
            own_send.at[j, way],
            pass_recv.at[j, way],
            peer,
        )

    def forward(j, way, peer):
        return remote(
            passing.at[j, way],
            yv.at[j, pl.ds(way * half, half)],
            fwd_send.at[j, way],
            fwd_recv.at[j, way],
            peer,
        )

    def direct(j):
        return remote(x_hbm.at[:, columns(j)], yv.at[j], fwd_send.at[j, 0], fwd_recv.at[j, 0], partner)

    a_load(0).start()
    a_load(1).start()
    pl.semaphore_wait(barrier, len(peers))

    if relay:
        for j in range(2):
            for way, peer in ways:
                own(j, way, peer).start()
    else:
        for j in range(chunks):
            direct(j).start()

    def start_x(j, _):
        x_load(j).start()
        return 0

    lax.fori_loop(0, chunks, start_x, 0)

    pieces = width // STAGED

    def split_a(i, _):
        a_load(i).wait()
        slot = lax.rem(i, 2)
        here = pl.ds(pl.multiple_of(i * STAGED, STAGED), STAGED)
        value = staged[slot]
        high = value.astype(jnp.bfloat16)
        a_hi[here] = high
        a_lo[here] = (value - high.astype(jnp.float32)).astype(jnp.bfloat16)

        @pl.when(i + 2 < pieces)
        def _():
            a_load(i + 2).start()

        return 0

    lax.fori_loop(0, pieces, split_a, 0)

    def core_copy(j, first, count):
        return remote(
            prod.at[j, pl.ds(first, count), 1 - core],
            core_in.at[j, pl.ds(first, count)],
            core_send.at[j],
            core_recv.at[j],
            sibling,
        )

    groups = prod.shape[1]
    step_groups = ROWS_AT_ONCE // LANES

    def relay_step(j):
        for way, peer in ways:
            own(j, way, peer).wait_recv()
            forward(j, way, peer).start()

        @pl.when(j + 2 < chunks)
        def _():
            for way, peer in ways:
                own(j + 2, way, peer).start()

    def multiply(j):
        x_load(j).wait()
        if relay:
            for way, peer in ways:
                forward(j, way, peer).wait_recv()
        else:
            direct(j).wait_recv()
        combined = yv[j] + sign * xv[j]
        high = combined.astype(jnp.bfloat16)
        b_parts[:, :LANES] = high
        b_parts[:, LANES:] = (combined - high.astype(jnp.float32)).astype(jnp.bfloat16)

        def rows_step(m, _):
            here = pl.ds(pl.multiple_of(m * ROWS_AT_ONCE, ROWS_AT_ONCE), ROWS_AT_ONCE)
            main = jnp.dot(a_hi[here], b_parts[...], preferred_element_type=jnp.float32)
            rest = jnp.dot(a_lo[here], b_parts[:, :LANES], preferred_element_type=jnp.float32)
            total = main[:, :LANES] + (main[:, LANES:] + rest)
            first = m * step_groups
            prod[j, pl.ds(first, step_groups)] = total.reshape(step_groups, 2, n_y, rows, LANES)
            core_copy(j, first, step_groups).start()
            return 0

        lax.fori_loop(0, width // ROWS_AT_ONCE, rows_step, 0)

    def y_copy(j, d):
        return remote(
            prod.at[j, :, core, lax.rem(y + d, n_y)], y_in.at[j, n_y - 1 - d], y_send.at[j], y_recv.at[j], y_peers[d - 1]
        )

    def y_all(j):
        return remote(y_in.at[j], y_in.at[j], y_send.at[j], y_recv.at[j], y_peers[0])

    def z_copy(j, d):
        return remote(
            s2.at[j, :, lax.rem(z + d, n_z)], z_in.at[j, n_z - 1 - d], z_send.at[j], z_recv.at[j], z_peers[d - 1]
        )

    def z_all(j):
        return remote(z_in.at[j], z_in.at[j], z_send.at[j], z_recv.at[j], z_peers[0])

    def far_copy(j, k):
        column = 1 - xlo if k != 1 else xlo
        return remote(s3.at[j, column], far_in.at[j, k], far_send.at[j], far_recv.at[j], far_peers[k])

    def far_all(j):
        return remote(far_in.at[j], far_in.at[j], far_send.at[j], far_recv.at[j], far_peers[0])

    def after_core(j):
        core_copy(j, 0, groups).wait_recv()
        prod[j, :, core] = prod[j, :, core] + core_in[j]
        for d in range(1, n_y):
            y_copy(j, d).start()

    def after_y(j):
        y_all(j).wait_recv()
        total = prod[j, :, core, y]
        for d in range(n_y - 1):
            total = total + y_in[j, d]
        s2[j] = total.reshape(s2.shape[1:])
        for d in range(1, n_z):
            z_copy(j, d).start()

    def after_z(j):
        z_all(j).wait_recv()
        total = s2[j, :, z]
        for d in range(n_z - 1):
            total = total + z_in[j, d]
        s3[j] = total
        for k in range(3):
            far_copy(j, k).start()

    def after_far(j):
        far_all(j).wait_recv()
        mine = s3[j, xlo] + far_in[j, 0]
        other = far_in[j, 1] + far_in[j, 2]
        out_ref[:, columns(j)] = 0.5 * (other + sign * mine)

    lag = 1 if relay else 0

    def step(t, _):
        for stage, delay in ((after_core, 1), (after_y, 2), (after_z, 3), (after_far, 4)):
            j = t - lag - delay

            @pl.when((j >= 0) & (j < chunks))
            def _(stage=stage, j=j):
                stage(j)

        if relay:

            @pl.when(t < chunks)
            def _():
                relay_step(t)

        @pl.when((t >= lag) & (t - lag < chunks))
        def _():
            multiply(t - lag)

        return 0

    lax.fori_loop(0, chunks + lag + 4, step, 0)

    def drain(j, _):
        if relay:
            for way, peer in ways:
                own(j, way, peer).wait_send()
                forward(j, way, peer).wait_send()
        else:
            direct(j).wait_send()
        core_copy(j, 0, groups).wait_send()
        y_all(j).wait_send()
        z_all(j).wait_send()
        far_all(j).wait_send()
        return 0

    lax.fori_loop(0, chunks, drain, 0)


def shards(relay, tiles, trial):
    matrix, block = tiles[0], trial[0]
    width, depth = matrix.shape
    n = block.shape[1]
    n_z, n_y = lax.axis_size("z"), lax.axis_size("y")
    owners = lax.axis_size(OWNERS)
    rows = width // owners
    chunks = n // LANES
    groups = owners // (2 * n_y)
    f32, bf16 = jnp.float32, jnp.bfloat16
    dma = pltpu.SemaphoreType.DMA
    result = pl.pallas_call(
        functools.partial(kernel, n_z, n_y, rows, relay),
        out_shape=jax.ShapeDtypeStruct((rows, n), f32),
        in_specs=[pl.BlockSpec(memory_space=pl.ANY)] * 2,
        out_specs=pl.BlockSpec(memory_space=pltpu.VMEM),
        scratch_shapes=[
            pltpu.VMEM((chunks, depth, LANES), f32),
            pltpu.VMEM((chunks, depth, LANES), f32),
            pltpu.VMEM((chunks, 2, depth // 2, LANES), f32),
            pltpu.VMEM((width, depth), bf16),
            pltpu.VMEM((width, depth), bf16),
            pltpu.VMEM((2, STAGED, depth), f32),
            pltpu.VMEM((depth, 2 * LANES), bf16),
            pltpu.VMEM((chunks, groups, 2, n_y, rows, LANES), f32),
            pltpu.VMEM((chunks, groups, n_y, rows, LANES), f32),
            pltpu.VMEM((chunks, n_y - 1, groups, rows, LANES), f32),
            pltpu.VMEM((chunks, 2, n_z, rows, LANES), f32),
            pltpu.VMEM((chunks, n_z - 1, 2, rows, LANES), f32),
            pltpu.VMEM((chunks, 2, rows, LANES), f32),
            pltpu.VMEM((chunks, 3, rows, LANES), f32),
            dma((chunks,)),
            dma((2,)),
            *[dma((chunks, 2))] * 4,
            *[dma((chunks,))] * 8,
        ],
        compiler_params=pltpu.CompilerParams(
            collective_id=0, has_side_effects=True, vmem_limit_bytes=60 * 2**20
        ),
    )(matrix, block)
    return result[None]


RELAY = True


def solution(mesh):
    blk = mesh.shape["blk"]
    split = Mesh(
        mesh.devices.reshape(mesh.shape["pair"], 2, blk // 4, 2, mesh.shape["rows"]),
        AXES,
    )
    return jax.shard_map(
        functools.partial(shards, RELAY),
        mesh=split,
        in_specs=(P("pair", None, OWNERS), P("pair", OWNERS, None)),
        out_specs=P("pair", OWNERS, None),
        check_vma=False,
    )
```

time: 317 us -> 127 us (0.40)
  waiting for transfers between devices: 221 us -> 0 us
  Pallas kernels: 0 us -> 124 us
  matrix products: 57.8 us -> 0 us
  local copies, waits for them, and re-layouts: 17.5 us -> 1.47 us
  between operations: 13.1 us -> 0.01 us
  starting transfers between devices: 5.83 us -> 0 us
    reduce_scatter x4 -> x0, waiting for transfers between devices: 127 us -> none  [own_block_2(): pieces = lax.psum_scatter(pieces, axes[k], scatter_dimension=0, tiled=True)]
    pallas_call x0 -> x1, Pallas kernels: none -> 124 us  [shards(): pl.pallas_call(functools.partial(kernel, n_z, n_y, rows, relay), out_shap...]
    ppermute x2 -> x0, waiting for transfers between devices: 94.4 us -> none  [swapped(): return lax.ppermute(value, axis, pairs)]
    dot_general x1 -> x0, matrix products: 57.8 us -> none  [shards(): jnp.dot(matrix, combined, precision=lax.Precision.HIGHEST, preferred_elem...]
    dot_general x1 -> x0, local copies, waits for them, and re-layouts: 9.25 us -> none  [shards(): jnp.dot(matrix, combined, precision=lax.Precision.HIGHEST, preferred_elem...]
    transpose x1 -> x0, local copies, waits for them, and re-layouts: 8.27 us -> none  [own_block_2(): pieces = jnp.moveaxis(pieces, turns, range(len(axes))).reshape(-1, *inside)]
    ppermute x2 -> x0, starting transfers between devices: 5.71 us -> none  [swapped(): return lax.ppermute(value, axis, pairs)]
  transfers between devices with their start and end apart: 6 -> 0, of which waited for: 6 -> 0; matrix products, arithmetic and copies ran while one was open for 0% -> 0% of each run, Pallas kernels for 0% -> 0%
where the time goes in v1:
time: 127 us; the launch traced here: 126 us
  Pallas kernels  124 us (98%)
  local copies, waits for them, and re-layouts  1.47 us (1%)
    pallas_call x1, Pallas kernels, shards(): pl.pallas_call(functools.partial(kernel, n_z, n_y, rows, relay), out_shap...  124 us

profile of v1, /device:TPU:8, one launch (start us, length us, event | category | flops | bytes accessed | tf_op | source)
XLA Modules:
  0.0 125.9 jit_solution(13572829404488061402)
XLA Ops:
  0.0 124.4 %shard_map.28 = f32[16,1024]{1,0:T(8,128)} custom-call(f32[2048,1024]{1,0:T(8,128)} %bitcast.3, f32[1024,1024]{1,0:T(8,128)} %bitcast.4), custom_call_target="tpu_custom_call" | custom-call | tf_op jit(solution)/shard_map/pallas_call | solution.py:281
  124.4 1.5 %copy.4 = f32[1,16,1024]{2,1,0:T(8,128)} copy(f32[1,16,1024]{2,1,0:T(8,128)} %bitcast.5) | data formatting | bytes 131072

commit v2 on v0

v2 whole, which is shorter than its diff:
```python
import functools

import jax
import jax.numpy as jnp
from jax import lax
from jax.experimental import pallas as pl
from jax.experimental.pallas import tpu as pltpu
from jax.sharding import Mesh
from jax.sharding import PartitionSpec as P

MESH = pl.DeviceIdType.MESH
AXES = ("pair", "xlo", "z", "core", "y")
OWNERS = ("xlo", "z", "core", "y")
LANES = 128
ROWS_AT_ONCE = 512
STAGED = 256


class Part:
    def __init__(self, at, refs):
        names = (
            "prod", "core_in", "y_in", "s2", "z_in", "s3", "far_in",
            "core_send", "core_recv", "y_send", "y_recv", "z_send", "z_recv", "far_send", "far_recv",
        )
        for name, ref in zip(names, refs):
            setattr(self, name, ref.at[at])


def kernel(n_z, n_y, rows, a_hbm, x_hbm, out_ref, *scratch):
    (xv, yv, xt, yt, a_hi, a_lo, staged, b_parts, acc) = scratch[:9]
    full, last = scratch[9:16], scratch[16:23]
    x_sem, a_sem, full_send, full_recv, last_send, last_recv = scratch[23:29]
    full, last = full + scratch[29:37], last + scratch[37:45]

    p, xlo, z, core, y = (lax.axis_index(a) for a in AXES)
    chunks = yv.shape[0]
    depth, width = a_hbm.shape[1], a_hbm.shape[0]
    half = depth // 2
    fine = xt.shape[2]
    sign = 1.0 - 2.0 * p.astype(jnp.float32)

    partner = {"pair": 1 - p}
    sibling = {"core": 1 - core}
    y_peers = [{"y": lax.rem(y + d, n_y)} for d in range(1, n_y)]
    z_peers = [{"z": lax.rem(z + d, n_z)} for d in range(1, n_z)]
    far_peers = [
        {"xlo": 1 - xlo},
        {"pair": 1 - p},
        {"pair": 1 - p, "xlo": 1 - xlo},
    ]
    peers = [sibling, *y_peers, *z_peers, *far_peers]

    barrier = pltpu.get_barrier_semaphore()
    for peer in peers:
        pl.semaphore_signal(barrier, inc=1, device_id=peer, device_id_type=MESH)

    def columns(j):
        return pl.ds(pl.multiple_of(j * LANES, LANES), LANES)

    def x_load(j):
        return pltpu.make_async_copy(x_hbm.at[:, columns(j)], xv.at[j], x_sem.at[j])

    def a_load(i):
        slot = lax.rem(i, 2)
        return pltpu.make_async_copy(
            a_hbm.at[pl.ds(pl.multiple_of(i * STAGED, STAGED), STAGED)], staged.at[slot], a_sem.at[slot]
        )

    def remote(src, dst, send, recv, peer):
        return pltpu.make_async_remote_copy(
            src_ref=src, dst_ref=dst, send_sem=send, recv_sem=recv, device_id=peer, device_id_type=MESH
        )

    def exchange(j, q):
        here = pl.ds(q * half, half)
        return remote(x_hbm.at[here, columns(j)], yv.at[j, here], full_send.at[j, q], full_recv.at[j, q], partner)

    def exchange_last(h):
        return remote(xt.at[h], yt.at[h], last_send.at[h], last_recv.at[h], partner)

    a_load(0).start()
    a_load(1).start()
    pl.semaphore_wait(barrier, len(peers))

    for q in range(2):
        exchange(0, q).start()

    def start_x(j, _):
        x_load(j).start()
        return 0

    lax.fori_loop(0, chunks + 1, start_x, 0)

    pieces = width // STAGED

    def split_a(i, _):
        a_load(i).wait()
        slot = lax.rem(i, 2)
        here = pl.ds(pl.multiple_of(i * STAGED, STAGED), STAGED)
        value = staged[slot]
        high = value.astype(jnp.bfloat16)
        a_hi[here] = high
        a_lo[here] = (value - high.astype(jnp.float32)).astype(jnp.bfloat16)

        @pl.when(i + 2 < pieces)
        def _():
            a_load(i + 2).start()

        return 0

    lax.fori_loop(0, pieces, split_a, 0)

    def turned(value):
        return pltpu.roll(value, LANES // 2, 1)

    def lower_half(shape):
        return lax.broadcasted_iota(jnp.int32, shape, len(shape) - 1) < LANES // 2

    x_load(chunks).wait()
    narrow = lower_half((fine, LANES))
    for b in range(4):
        upper = xv[chunks, pl.ds(2 * b * fine, fine)]
        lower = xv[chunks, pl.ds((2 * b + 1) * fine, fine)]
        xt[0, b] = jnp.where(narrow, upper, turned(lower))
        xt[1, b] = jnp.where(narrow, turned(upper), lower)

    groups = full[0].shape[1]
    blocks = width // ROWS_AT_ONCE
    step_groups = groups // blocks

    def core_copy(r, m):
        part = pl.ds(m * step_groups, step_groups)
        return remote(r.prod.at[part, 1 - core], r.core_in.at[part], r.core_send.at[m], r.core_recv.at[m], sibling)

    def multiply(j, q):
        exchange(j, q).wait_recv()
        later = j + 1 < chunks

        @pl.when(later)
        def _():
            exchange(j + 1, q).start()

        @pl.when(jnp.logical_not(later))
        def _():
            exchange_last(q).start()

        ks = pl.ds(q * half, half)
        combined = yv[j, ks] + sign * xv[j, ks]
        high = combined.astype(jnp.bfloat16)
        b_parts[ks, :LANES] = high
        b_parts[ks, LANES:] = (combined - high.astype(jnp.float32)).astype(jnp.bfloat16)
        r = Part(j, full)

        def rows_step(m, _):
            here = pl.ds(pl.multiple_of(m * ROWS_AT_ONCE, ROWS_AT_ONCE), ROWS_AT_ONCE)
            main = jnp.dot(a_hi[here, ks], b_parts[ks], preferred_element_type=jnp.float32)
            rest = jnp.dot(a_lo[here, ks], b_parts[ks, :LANES], preferred_element_type=jnp.float32)
            total = main[:, :LANES] + (main[:, LANES:] + rest)
            if q == 0:
                acc[here] = total
            else:
                total = total + acc[here]
                r.prod[pl.ds(m * step_groups, step_groups)] = total.reshape(step_groups, 2, n_y, rows, LANES)
                core_copy(r, m).start()
            return 0

        lax.fori_loop(0, blocks, rows_step, 0)

    def prepare_last(h):
        exchange_last(h).wait_recv()
        for b in range(4):
            combined = yt[h, b] + sign * xt[h, b]
            high = combined.astype(jnp.bfloat16).astype(jnp.float32)
            low = combined - high
            high_t, low_t = turned(high), turned(low)
            upper = pl.ds(2 * b * fine, fine)
            lower = pl.ds((2 * b + 1) * fine, fine)
            b_parts[upper, :LANES] = jnp.where(narrow, high, low_t).astype(jnp.bfloat16)
            b_parts[upper, LANES:] = jnp.where(narrow, high, high_t).astype(jnp.bfloat16)
            b_parts[lower, :LANES] = jnp.where(narrow, high_t, low).astype(jnp.bfloat16)
            b_parts[lower, LANES:] = jnp.where(narrow, high_t, high).astype(jnp.bfloat16)

    def multiply_last(r, m):
        here = pl.ds(pl.multiple_of(m * ROWS_AT_ONCE, ROWS_AT_ONCE), ROWS_AT_ONCE)
        main = jnp.dot(a_hi[here], b_parts[:, :LANES], preferred_element_type=jnp.float32)
        rest = jnp.dot(a_lo[here], b_parts[:, LANES:], preferred_element_type=jnp.float32)
        total = main + (turned(main) + rest)
        total = total.reshape(step_groups, 2, n_y, 2, rows // 2, LANES)
        packed = jnp.where(lower_half((step_groups, 2, n_y, rows // 2, LANES)), total[:, :, :, 0], total[:, :, :, 1])
        r.prod[pl.ds(m * step_groups, step_groups)] = packed
        core_copy(r, m).start()

    def y_copy(r, part, d):
        src = r.prod.at[part, core, lax.rem(y + d, n_y)]
        return remote(src, r.y_in.at[n_y - 1 - d, part], r.y_send, r.y_recv, y_peers[d - 1])

    def y_all(r):
        return remote(r.y_in, r.y_in, r.y_send, r.y_recv, y_peers[0])

    def z_copy(r, d):
        return remote(r.s2.at[:, lax.rem(z + d, n_z)], r.z_in.at[n_z - 1 - d], r.z_send, r.z_recv, z_peers[d - 1])

    def z_all(r):
        return remote(r.z_in, r.z_in, r.z_send, r.z_recv, z_peers[0])

    def far_copy(r, k):
        column = 1 - xlo if k != 1 else xlo
        return remote(r.s3.at[column], r.far_in.at[k], r.far_send, r.far_recv, far_peers[k])

    def far_all(r):
        return remote(r.far_in, r.far_in, r.far_send, r.far_recv, far_peers[0])

    def after_core(r, first=0, count=blocks):
        for m in range(first, first + count):
            core_copy(r, m).wait_recv()
        part = pl.ds(first * step_groups, count * step_groups)
        r.prod[part, core] = r.prod[part, core] + r.core_in[part]
        for d in range(1, n_y):
            y_copy(r, part, d).start()

    def after_y(r):
        y_all(r).wait_recv()
        total = r.prod[:, core, y]
        for d in range(n_y - 1):
            total = total + r.y_in[d]
        r.s2[...] = total.reshape(r.s2.shape)
        for d in range(1, n_z):
            z_copy(r, d).start()

    def after_z(r):
        z_all(r).wait_recv()
        total = r.s2[:, z]
        for d in range(n_z - 1):
            total = total + r.z_in[d]
        r.s3[...] = total
        for k in range(3):
            far_copy(r, k).start()

    def after_far(r):
        far_all(r).wait_recv()
        mine = r.s3[xlo] + r.far_in[0]
        other = r.far_in[1] + r.far_in[2]
        return 0.5 * (other + sign * mine)

    def finish(j):
        out_ref[:, columns(j)] = after_far(Part(j, full))

    def step(j, _):
        @pl.when(j >= 1)
        def _():
            after_core(Part(j - 1, full))

        x_load(j).wait()
        multiply(j, 0)
        for stage, delay in ((after_y, 2), (after_z, 3)):

            @pl.when(j >= delay)
            def _(stage=stage, at=j - delay):
                stage(Part(at, full))

        @pl.when(j >= 4)
        def _():
            finish(j - 4)

        multiply(j, 1)
        return 0

    lax.fori_loop(0, chunks, step, 0)

    f = [Part(j, full) for j in range(chunks)]
    e = [Part(h, last) for h in range(2)]
    n = chunks
    after_core(f[n - 1])
    after_y(f[n - 2])
    after_z(f[n - 3])
    finish(n - 4)
    prepare_last(0)

    def rows_step(m, _):
        multiply_last(e[0], m)
        return 0

    lax.fori_loop(0, blocks, rows_step, 0)
    prepare_last(1)
    multiply_last(e[1], 0)
    after_core(e[0])
    multiply_last(e[1], 1)
    after_core(e[1], 0, 1)
    after_y(f[n - 1])
    multiply_last(e[1], 2)
    after_core(e[1], 1, 1)
    multiply_last(e[1], 3)
    after_core(e[1], 2, 1)
    after_z(f[n - 2])
    finish(n - 3)
    after_core(e[1], 3, 1)
    after_y(e[0])
    after_y(e[1])
    after_z(f[n - 1])
    after_z(e[0])
    finish(n - 2)
    after_z(e[1])
    finish(n - 1)
    first_half, second_half = after_far(e[0]), after_far(e[1])
    narrow = lower_half((rows // 2, LANES))
    at = pl.ds(n * LANES, LANES)
    out_ref[: rows // 2, at] = jnp.where(narrow, first_half, turned(second_half))
    out_ref[rows // 2 :, at] = jnp.where(narrow, turned(first_half), second_half)

    def sent(r):
        for m in range(blocks):
            core_copy(r, m).wait_send()
        y_all(r).wait_send()
        z_all(r).wait_send()
        far_all(r).wait_send()

    def drain(j, _):
        for q in range(2):
            exchange(j, q).wait_send()
        sent(Part(j, full))
        return 0

    lax.fori_loop(0, chunks, drain, 0)
    for h in range(2):
        exchange_last(h).wait_send()
    for h in range(2):
        sent(e[h])


def shards(tiles, trial):
    matrix, block = tiles[0], trial[0]
    width, depth = matrix.shape
    n = block.shape[1]
    n_z, n_y = lax.axis_size("z"), lax.axis_size("y")
    owners = lax.axis_size(OWNERS)
    rows = width // owners
    chunks = n // LANES - 1
    groups = owners // (2 * n_y)
    fine = depth // 8
    f32, bf16 = jnp.float32, jnp.bfloat16
    dma = pltpu.SemaphoreType.DMA

    def reduction(count, height):
        return [
            pltpu.VMEM((count, groups, 2, n_y, height, LANES), f32),
            pltpu.VMEM((count, groups, n_y, height, LANES), f32),
            pltpu.VMEM((count, n_y - 1, groups, height, LANES), f32),
            pltpu.VMEM((count, 2, n_z, height, LANES), f32),
            pltpu.VMEM((count, n_z - 1, 2, height, LANES), f32),
            pltpu.VMEM((count, 2, height, LANES), f32),
            pltpu.VMEM((count, 3, height, LANES), f32),
        ]

    result = pl.pallas_call(
        functools.partial(kernel, n_z, n_y, rows),
        out_shape=jax.ShapeDtypeStruct((rows, n), f32),
        in_specs=[pl.BlockSpec(memory_space=pl.ANY)] * 2,
        out_specs=pl.BlockSpec(memory_space=pltpu.VMEM),
        scratch_shapes=[
            pltpu.VMEM((chunks + 1, depth, LANES), f32),
            pltpu.VMEM((chunks, depth, LANES), f32),
            *[pltpu.VMEM((2, 4, fine, LANES), f32)] * 2,
            pltpu.VMEM((width, depth), bf16),
            pltpu.VMEM((width, depth), bf16),
            pltpu.VMEM((2, STAGED, depth), f32),
            pltpu.VMEM((depth, 2 * LANES), bf16),
            pltpu.VMEM((width, LANES), f32),
            *reduction(chunks, rows),
            *reduction(2, rows // 2),
            dma((chunks + 1,)),
            dma((2,)),
            *[dma((chunks, 2))] * 2,
            *[dma((2,))] * 2,
            *[dma((chunks, width // ROWS_AT_ONCE))] * 2,
            *[dma((chunks,))] * 6,
            *[dma((2, width // ROWS_AT_ONCE))] * 2,
            *[dma((2,))] * 6,
        ],
        compiler_params=pltpu.CompilerParams(
            collective_id=0, has_side_effects=True, vmem_limit_bytes=60 * 2**20
        ),
    )(matrix, block)
    return result[None]


def solution(mesh):
    blk = mesh.shape["blk"]
    split = Mesh(
        mesh.devices.reshape(mesh.shape["pair"], 2, blk // 4, 2, mesh.shape["rows"]),
        AXES,
    )
    return jax.shard_map(
        shards,
        mesh=split,
        in_specs=(P("pair", None, OWNERS), P("pair", OWNERS, None)),
        out_specs=P("pair", OWNERS, None),
        check_vma=False,
    )
```

time: 317 us -> 122 us (0.38)
  waiting for transfers between devices: 221 us -> 0 us
  Pallas kernels: 0 us -> 121 us
  matrix products: 57.8 us -> 0 us
  local copies, waits for them, and re-layouts: 17.5 us -> 1.47 us
  between operations: 13.1 us -> 0.01 us
  starting transfers between devices: 5.83 us -> 0 us
    reduce_scatter x4 -> x0, waiting for transfers between devices: 127 us -> none  [own_block_2(): pieces = lax.psum_scatter(pieces, axes[k], scatter_dimension=0, tiled=True)]
    pallas_call x0 -> x1, Pallas kernels: none -> 121 us  [shards(): pl.pallas_call(functools.partial(kernel, n_z, n_y, rows), out_shape=jax.S...]
    ppermute x2 -> x0, waiting for transfers between devices: 94.4 us -> none  [swapped(): return lax.ppermute(value, axis, pairs)]
    dot_general x1 -> x0, matrix products: 57.8 us -> none  [shards(): jnp.dot(matrix, combined, precision=lax.Precision.HIGHEST, preferred_elem...]
    dot_general x1 -> x0, local copies, waits for them, and re-layouts: 9.25 us -> none  [shards(): jnp.dot(matrix, combined, precision=lax.Precision.HIGHEST, preferred_elem...]
    transpose x1 -> x0, local copies, waits for them, and re-layouts: 8.27 us -> none  [own_block_2(): pieces = jnp.moveaxis(pieces, turns, range(len(axes))).reshape(-1, *inside)]
    ppermute x2 -> x0, starting transfers between devices: 5.71 us -> none  [swapped(): return lax.ppermute(value, axis, pairs)]
  transfers between devices with their start and end apart: 6 -> 0, of which waited for: 6 -> 0; matrix products, arithmetic and copies ran while one was open for 0% -> 0% of each run, Pallas kernels for 0% -> 0%
where the time goes in v2:
time: 122 us
  Pallas kernels  121 us (99%)
  local copies, waits for them, and re-layouts  1.47 us (1%)
    pallas_call x1, Pallas kernels, shards(): pl.pallas_call(functools.partial(kernel, n_z, n_y, rows), out_shape=jax.S...  121 us

profile of v2, /device:TPU:8, one launch (start us, length us, event | category | flops | bytes accessed | tf_op | source)
XLA Modules:
  0.0 122.3 jit_solution(17149957716296986039)
XLA Ops:
  0.0 120.8 %shard_map.28 = f32[16,1024]{1,0:T(8,128)} custom-call(f32[2048,1024]{1,0:T(8,128)} %bitcast.3, f32[1024,1024]{1,0:T(8,128)} %bitcast.4), custom_call_target="tpu_custom_call" | custom-call | tf_op jit(solution)/shard_map/pallas_call | solution.py:354
  120.8 1.5 %copy.4 = f32[1,16,1024]{2,1,0:T(8,128)} copy(f32[1,16,1024]{2,1,0:T(8,128)} %bitcast.5) | data formatting | bytes 131072

commit v3 on v2

--- a/solution.py
+++ b/solution.py
@@ -227,14 +227,20 @@
         for d in range(1, n_z):
             z_copy(r, d).start()
 
-    def after_z(r):
+    def sum_z(r):
         z_all(r).wait_recv()
         total = r.s2[:, z]
         for d in range(n_z - 1):
             total = total + r.z_in[d]
         r.s3[...] = total
+
+    def send_far(r):
         for k in range(3):
             far_copy(r, k).start()
+
+    def after_z(r):
+        sum_z(r)
+        send_far(r)
 
     def after_far(r):
         far_all(r).wait_recv()
@@ -252,18 +258,19 @@
 
         x_load(j).wait()
         multiply(j, 0)
-        for stage, delay in ((after_y, 2), (after_z, 3)):
+        for stage, delay in ((after_y, 2), (sum_z, 3)):
 
             @pl.when(j >= delay)
             def _(stage=stage, at=j - delay):
                 stage(Part(at, full))
 
-        @pl.when(j >= 4)
-        def _():
-            finish(j - 4)
-
         multiply(j, 1)
         return 0
+
+    def sent(r):
+        for m in range(blocks):
+            core_copy(r, m).wait_send()
+        y_all(r).wait_send()
 
     lax.fori_loop(0, chunks, step, 0)
 
@@ -272,59 +279,74 @@
     n = chunks
     after_core(f[n - 1])
     after_y(f[n - 2])
-    after_z(f[n - 3])
-    finish(n - 4)
+    sum_z(f[n - 3])
     prepare_last(0)
 
-    def rows_step(m, _):
-        multiply_last(e[0], m)
-        return 0
-
-    lax.fori_loop(0, blocks, rows_step, 0)
+    def early_far(j, _):
+        send_far(Part(j, full))
+        return 0
+
+    def early_finish(j, _):
+        finish(j)
+        return 0
+
+    multiply_last(e[0], 0)
+    multiply_last(e[0], 1)
+    after_core(e[0], 0, 1)
+    multiply_last(e[0], 2)
+    after_core(e[0], 1, 1)
+    multiply_last(e[0], 3)
+    after_core(e[0], 2, 1)
     prepare_last(1)
     multiply_last(e[1], 0)
-    after_core(e[0])
+    after_core(e[0], 3, 1)
     multiply_last(e[1], 1)
     after_core(e[1], 0, 1)
-    after_y(f[n - 1])
     multiply_last(e[1], 2)
     after_core(e[1], 1, 1)
     multiply_last(e[1], 3)
     after_core(e[1], 2, 1)
-    after_z(f[n - 2])
-    finish(n - 3)
+    after_y(f[n - 1])
     after_core(e[1], 3, 1)
     after_y(e[0])
+    after_z(f[n - 2])
+    lax.fori_loop(0, n - 2, early_far, 0)
     after_y(e[1])
+    lax.fori_loop(0, n - 2, early_finish, 0)
     after_z(f[n - 1])
     after_z(e[0])
+
+    def drain(j, _):
+        for q in range(2):
+            exchange(j, q).wait_send()
+        r = Part(j, full)
+        sent(r)
+        z_all(r).wait_send()
+        return 0
+
+    lax.fori_loop(0, chunks, drain, 0)
+    for h in range(2):
+        exchange_last(h).wait_send()
+        sent(e[h])
+    z_all(e[0]).wait_send()
+    after_z(e[1])
     finish(n - 2)
-    after_z(e[1])
     finish(n - 1)
-    first_half, second_half = after_far(e[0]), after_far(e[1])
+
+    def drain_far(j, _):
+        far_all(Part(j, full)).wait_send()
+        return 0
+
+    lax.fori_loop(0, chunks, drain_far, 0)
+    far_all(e[0]).wait_send()
+    z_all(e[1]).wait_send()
+    first_half = after_far(e[0])
+    second_half = after_far(e[1])
     narrow = lower_half((rows // 2, LANES))
     at = pl.ds(n * LANES, LANES)
     out_ref[: rows // 2, at] = jnp.where(narrow, first_half, turned(second_half))
     out_ref[rows // 2 :, at] = jnp.where(narrow, turned(first_half), second_half)
-
-    def sent(r):
-        for m in range(blocks):
-            core_copy(r, m).wait_send()
-        y_all(r).wait_send()
-        z_all(r).wait_send()
-        far_all(r).wait_send()
-
-    def drain(j, _):
-        for q in range(2):
-            exchange(j, q).wait_send()
-        sent(Part(j, full))
-        return 0
-
-    lax.fori_loop(0, chunks, drain, 0)
-    for h in range(2):
-        exchange_last(h).wait_send()
-    for h in range(2):
-        sent(e[h])
+    far_all(e[1]).wait_send()
 
 
 def shards(tiles, trial):
@@ -353,7 +375,7 @@
 
     result = pl.pallas_call(
         functools.partial(kernel, n_z, n_y, rows),
-        out_shape=jax.ShapeDtypeStruct((rows, n), f32),
+        out_shape=pltpu.VMEM((rows, n), f32),
         in_specs=[pl.BlockSpec(memory_space=pl.ANY)] * 2,
         out_specs=pl.BlockSpec(memory_space=pltpu.VMEM),
         scratch_shapes=[

time: 122 us -> 119 us (0.975)
  Pallas kernels: 121 us -> 118 us
    pallas_call x1, Pallas kernels: 121 us -> 118 us  [shards(): pl.pallas_call(functools.partial(kernel, n_z, n_y, rows), out_shape=pltpu...]
where the time goes in v3:
time: 119 us
  Pallas kernels  118 us (99%)
    pallas_call x1, Pallas kernels, shards(): pl.pallas_call(functools.partial(kernel, n_z, n_y, rows), out_shape=pltpu...  118 us

profile of v3, /device:TPU:8, one launch (start us, length us, event | category | flops | bytes accessed | tf_op | source)
XLA Modules:
  0.0 119.0 jit_solution(6772315006446403186)
XLA Ops:
  0.0 118.3 %shard_map.28 = f32[16,1024]{1,0:T(8,128)S(1)} custom-call(f32[2048,1024]{1,0:T(8,128)} %bitcast.4, f32[1024,1024]{1,0:T(8,128)} %bitcast.5), custom_call_target="tpu_custom_call" | custom-call | tf_op jit(solution)/shard_map/pallas_call | solution.py:376
  118.4 0.6 copy.4

commit v4 on v3

--- a/solution.py
+++ b/solution.py
@@ -14,6 +14,10 @@
 LANES = 128
 ROWS_AT_ONCE = 512
 STAGED = 256
+
+
+def farthest_first(n):
+    return sorted(range(1, n), key=lambda d: -min(d, n - d))
 
 
 class Part:
@@ -215,7 +219,7 @@
             core_copy(r, m).wait_recv()
         part = pl.ds(first * step_groups, count * step_groups)
         r.prod[part, core] = r.prod[part, core] + r.core_in[part]
-        for d in range(1, n_y):
+        for d in farthest_first(n_y):
             y_copy(r, part, d).start()
 
     def after_y(r):
@@ -224,7 +228,7 @@
         for d in range(n_y - 1):
             total = total + r.y_in[d]
         r.s2[...] = total.reshape(r.s2.shape)
-        for d in range(1, n_z):
+        for d in farthest_first(n_z):
             z_copy(r, d).start()
 
     def sum_z(r):
@@ -235,7 +239,7 @@
         r.s3[...] = total
 
     def send_far(r):
-        for k in range(3):
+        for k in (1, 0, 2):
             far_copy(r, k).start()
 
     def after_z(r):

time: 119 us -> 119 us (level)
  no operation moved by 1% of the time
where the time goes in v4:
time: 119 us; the launch traced here: 118 us
  Pallas kernels  118 us (99%)
    pallas_call x1, Pallas kernels, shards(): pl.pallas_call(functools.partial(kernel, n_z, n_y, rows), out_shape=pltpu...  118 us

profile of v4, /device:TPU:8, one launch (start us, length us, event | category | flops | bytes accessed | tf_op | source)
XLA Modules:
  0.0 118.4 jit_solution(3956034946066306471)
XLA Ops:
  0.0 117.7 %shard_map.28 = f32[16,1024]{1,0:T(8,128)S(1)} custom-call(f32[2048,1024]{1,0:T(8,128)} %bitcast.4, f32[1024,1024]{1,0:T(8,128)} %bitcast.5), custom_call_target="tpu_custom_call" | custom-call | tf_op jit(solution)/shard_map/pallas_call | solution.py:380
  117.7 0.6 copy.4
